TPU v7x, 32 devices: a whole 2x2x4 slice. The times are simulated.
32 devices in a mesh: row: 16 (over z, x, core), col: 2 (over y).
Axes of the slice: x: 2, y: 2, z: 4, core: 2. Of those that a mesh axis runs over, the one named last changes fastest.
Arguments:
- x_train: bfloat16 [64, 8192], P(None, 'col'), may hold values from -8 to 8
- targets: float32 [8192], P('col'), may hold values from -6 to 6
- noise_draws: float32 [8192, 256], P('col', 'row'), may hold values from -3 to 3
- alpha_init: float32 [8192, 256], P('col', 'row'), may hold values from -6 to 6
- velocity_init: float32 [8192, 256], P('col', 'row'), may hold values from -3 to 3
- frequencies: bfloat16 [64, 4096], P(None, 'col'), may hold values from -5 to 5
- phases: float32 [4096], P('col'), may hold values from -3.140625 to 3.140625
- path_weights: bfloat16 [4096, 256], P('col'), may hold values from -6 to 6
- x_window: bfloat16 [64, 32768], P(None, 'row'), may hold values from -6 to 6
- batch_index: int32 [3, 8192], replicated, may hold values from 0 to 8191, as said below
Outputs:
- alpha_out: float32 [8192, 256], P('col', 'row')
- velocity_out: float32 [8192, 256], P('col', 'row')
- prior_window: float32 [256, 32768], P('col', 'row')
Inputs may be any that keep to these rules, and one draw needn't show every extreme that they name: `batch_index`: row b of every step names a training point of group g = (b // 256) % 2, that is a number from g * 4096 to (g + 1) * 4096 - 1; points may repeat.
All inputs are finite; a program needn't handle non-finite values.
Results may differ from a plain program's by a relative error of at most 0.0039.
Values may be sent and summed in bfloat16 or wider, within the bound.
A program may use at most 64 MiB of HBM per device.

v0:
```python
import jax
import jax.numpy as jnp
from jax import lax
from jax.sharding import PartitionSpec as P

FEAT = 4096
STEPS = 3


SQRT_THREE = 1.7320508075688772
LENGTH = 1.15
NOISE_VAR = 0.25
MOMENTUM = 0.9
STEP_SIZE = 0.5
HIGH = lax.Precision.HIGHEST


def features(points, frequencies, phases):
    phase_arg = lax.dot_general(
        frequencies, points, (((0,), (0,)), ((), ())), preferred_element_type=jnp.float32
    )
    factor = (2.0 / FEAT) ** 0.5
    return (factor * jnp.cos(phase_arg + phases[:, None])).astype(jnp.bfloat16)


def kernel_rows(points, x_train, train_norm):
    inner_prod = lax.dot_general(
        points, x_train, (((0,), (0,)), ((), ())), preferred_element_type=jnp.float32
    )
    point_norm = jnp.sum(jnp.square(points.astype(jnp.float32)), axis=0)
    dist_sq = jnp.maximum(point_norm[:, None] + train_norm[None, :] - 2.0 * inner_prod, 0.0)
    scaled = SQRT_THREE / LENGTH * jnp.sqrt(dist_sq)
    return ((1.0 + scaled) * jnp.exp(-scaled)).astype(jnp.bfloat16)


def shards(
    x_train,
    targets,
    noise_draws,
    alpha_init,
    velocity_init,
    frequencies,
    phases,
    path_weights,
    x_window,
    batch_index,
):
    row_count = lax.axis_size("row")
    col_count = lax.axis_size("col")
    row_id = lax.axis_index("row")
    col_id = lax.axis_index("col")
    train_cols = x_train.shape[1]
    batch_rows = batch_index.shape[1] // row_count
    own_rows = batch_rows // col_count
    col_start = col_id * train_cols
    my_index = lax.dynamic_slice_in_dim(batch_index, row_id * batch_rows, batch_rows, 1)
    flat_index = my_index.reshape(-1)
    column_ids = lax.broadcasted_iota(jnp.int32, (train_cols, 1), 0)
    selector = (column_ids == (flat_index - col_start)[None, :]).astype(jnp.bfloat16)
    picked = jnp.dot(x_train, selector, preferred_element_type=jnp.float32)
    batch_points = lax.psum(picked.astype(jnp.bfloat16), "col")
    phi_window = features(x_window, frequencies, phases)
    prior_window = lax.psum_scatter(
        lax.dot_general(
            path_weights, phi_window, (((0,), (0,)), ((), ())), preferred_element_type=jnp.float32
        ),
        "col",
        scatter_dimension=0,
        tiled=True,
    )
    train_norm = jnp.sum(jnp.square(x_train.astype(jnp.float32)), axis=0)
    block_rows = min(256, batch_rows)
    block_count = batch_rows // block_rows
    dual_state, velocity, noise_rows = (alpha_init, velocity_init, noise_draws)
    slot_ids = lax.broadcasted_iota(jnp.int32, (1, train_cols), 1)
    for step_id in range(STEPS):
        points_now = batch_points[:, step_id * batch_rows : (step_id + 1) * batch_rows]
        point_blocks = points_now.reshape(x_train.shape[0], block_count, block_rows).transpose(
            1, 0, 2
        )
        kernel_tile = lax.map(
            lambda block_points: kernel_rows(block_points, x_train, train_norm), point_blocks
        )
        kernel_tile = kernel_tile.reshape(batch_rows, train_cols)
        phi_batch = features(points_now, frequencies, phases)
        prior_rows = lax.dot_general(
            phi_batch, path_weights, (((0,), (0,)), ((), ())), preferred_element_type=jnp.float32
        )
        coeffs = dual_state.astype(jnp.bfloat16)
        coeffs = lax.all_gather(coeffs, "row", axis=1, tiled=True)
        coupled = jnp.dot(kernel_tile, coeffs, preferred_element_type=jnp.float32)
        partial_sum = coupled + prior_rows
        owned_rows = lax.psum_scatter(partial_sum, "col", scatter_dimension=0, tiled=True)
        arrived = lax.all_to_all(owned_rows, "row", split_axis=1, concat_axis=0, tiled=True)
        step_index = batch_index[step_id].reshape(row_count, col_count, own_rows)
        owner_slot = lax.dynamic_slice_in_dim(step_index, col_id, 1, 1).reshape(-1) - col_start
        owner_slot = jnp.clip(owner_slot, 0, train_cols - 1)
        point_terms = NOISE_VAR * dual_state - targets[:, None] + noise_rows
        owner_map = (owner_slot[:, None] == slot_ids).astype(jnp.float32)
        row_terms = arrived + jnp.dot(owner_map, point_terms, precision=HIGH)
        gradient = lax.dot_general(owner_map, row_terms, (((0,), (0,)), ((), ())), precision=HIGH)
        velocity = MOMENTUM * velocity - STEP_SIZE * gradient
        dual_state = dual_state + velocity
    return (dual_state, velocity, prior_window)


def solution(mesh):
    placed = (
        P(None, "col"),
        P("col"),
        P("col", "row"),
        P("col", "row"),
        P("col", "row"),
        P(None, "col"),
        P("col"),
        P("col", None),
        P(None, "row"),
        P(),
    )
    return jax.shard_map(
        shards,
        mesh=mesh,
        in_specs=placed,
        out_specs=(P("col", "row"), P("col", "row"), P("col", "row")),
        check_vma=False,
    )
```

profile of v0, /device:TPU:0, one launch (start us, length us, event | category | flops | bytes accessed | tf_op | source)
XLA Modules:
  0.0 538.4 jit_solution(8374524888942099227)
XLA Ops:
  8.9 6.0 %fusion.51 = bf16[64,1536]{1,0:T(8,128)(2,1)} fusion(bf16[64,4096]{1,0:T(8,128)(2,1)} %param.16, s32[1536]{0:T(1024)S(1)} %sub.84), kind=kOutput, calls=%fused_computation.69 | convolution fusion | flops 811696128 | bytes 727040 | tf_op jit(solution)/shard_map/dot_general | solution.py:60
  15.9 24.3 %all-reduce.2.cloned.1.call-done = bf16[64,1536]{1,0:T(8,128)(2,1)} async-done(((bf16[64,1536]{1,0:T(8,128)(2,1)}), bf16[64,1536]{1,0:T(8,128)(2,1)}) %all-reduce.2.cloned.1.call-update) | async-done | bytes 196624 | tf_op jit(solution)/shard_map/psum | solution.py:61
  43.6 8.4 %while.30 = (s32[]{:T(128)}, bf16[2,256,4096]{2,1,0:T(8,128)(2,1)}, bf16[2,64,256]{2,1,0:T(8,128)(2,1)S(1)}, f32[4096]{0:T(1024)S(1)}, bf16[64,4096]{1,0:T(8,128)(2,1)S(1)}, /*index=5*/s32[]{:T(128)}) while((s32[]{:T(128)}, bf16[2,256,4096]{2,1,0:T(8,128)(2,1)}, bf16[2,64,256]{2,1,0:T(8,128)(2,1)S(1)}, f32[4096]{0:T(1024)S(1)}, ...), condition=%wide.region_4.0_spmd, body=%wide.region_2.4_spmd.sunk | while | flops 143703808 | bytes 2706513 | solution.py:81
  52.0 10.3 %all-gather.4.cloned.1.call-done = bf16[4096,256]{0,1:T(8,128)(2,1)} async-done(((bf16[4096,16]{0,1:T(8,128)(2,1)}), bf16[4096,256]{0,1:T(8,128)(2,1)}) %all-gather.4.cloned.1.call-update) | async-done | bytes 2097168 | tf_op jit(solution)/shard_map/all_gather | solution.py:90
  67.3 29.4 %fusion.57 = f32[512,256]{1,0:T(8,128)} fusion(f32[512,256]{1,0:T(8,128)} %fusion.90, bf16[2048,256]{1,0:T(8,128)(2,1)S(1)} %copy-done, bf16[64,2048]{1,0:T(8,128)(2,1)S(1)} %copy-done.6, f32[2048]{0:T(1024)S(1)} %copy-done.10, bf16[64,1536]{1,0:T(8,128)(2,1)S(1)} %copy-done.3), kind=kOutput, calls=%fused_computation.75 | convolution fusion | flops 674365440 | bytes 2433024 | tf_op jit(solution)/shard_map/dot_general | solution.py:86
  96.7 13.5 %reduce-scatter.5.cloned.1.call-done = f32[256,256]{1,0:T(8,128)} async-done(((f32[512,256]{1,0:T(8,128)}), f32[256,256]{1,0:T(8,128)}) %reduce-scatter.5.cloned.1.call-update) | async-done | bytes 262160 | tf_op jit(solution)/shard_map/reduce_scatter | solution.py:93
  118.0 9.6 %all-to-all-done = f32[256,16,16]{0,2,1:T(8,128)S(1)} async-done(((f32[256,16,16]{0,2,1:T(8,128)}), f32[256,16,16]{0,2,1:T(8,128)S(1)}, u32[]{:S(2)}, u32[]{:S(2)}) %all-to-all-start) | async-done | bytes 262176 | tf_op jit(solution)/shard_map/all_to_all | solution.py:94
  127.7 30.4 %fusion.41 = f32[4096,16]{0,1:T(8,128)S(1)} fusion(f32[4096,16]{0,1:T(8,128)S(1)} %bitcast.131, s32[4096]{0:T(1024)S(1)} %bitcast.141, f32[4096,16]{0,1:T(8,128)S(1)} %copy-done.8, f32[4096,16]{0,1:T(8,128)S(1)} %copy-done.2, f32[4096]{0:T(1024)S(1)} %copy-done.9), kind=kOutput, calls=%fused_computation.55 | convolution fusion | flops 3238264832 | bytes 1081344 | tf_op jit(solution)/shard_map/dot_general | solution.py:100
  158.2 22.3 %fusion.87 = (bf16[4096,16]{0,1:T(8,128)(2,1)}, f32[4096,16]{0,1:T(8,128)S(1)}, f32[4096,16]{0,1:T(8,128)}) fusion(f32[4096,16]{0,1:T(8,128)S(1)} %copy-done.2, f32[4096,16]{0,1:T(8,128)S(1)} %fusion.41, s32[4096]{0:T(1024)S(1)} %bitcast.142, f32[4096,16]{0,1:T(8,128)S(1)} %copy-done.5), kind=kOutput, calls=%fused_computation.113 | convolution fusion | flops 3238330368 | bytes 1458176 | tf_op jit(solution)/shard_map/dot_general | solution.py:101
  183.0 8.5 %while.31 = (s32[]{:T(128)}, bf16[2,256,4096]{2,1,0:T(8,128)(2,1)}, bf16[2,64,256]{2,1,0:T(8,128)(2,1)S(1)}, f32[4096]{0:T(1024)S(1)}, bf16[64,4096]{1,0:T(8,128)(2,1)S(1)}, /*index=5*/s32[]{:T(128)}) while((s32[]{:T(128)}, bf16[2,256,4096]{2,1,0:T(8,128)(2,1)}, bf16[2,64,256]{2,1,0:T(8,128)(2,1)S(1)}, f32[4096]{0:T(1024)S(1)}, ...), condition=%wide.region_8.9_spmd, body=%wide.region_6.8_spmd.sunk | while | flops 143703808 | bytes 2706513 | solution.py:81
  191.5 27.8 %all-gather.6.cloned.1.call-done = bf16[4096,256]{0,1:T(8,128)(2,1)} async-done(((bf16[4096,16]{0,1:T(8,128)(2,1)}), bf16[4096,256]{0,1:T(8,128)(2,1)}) %all-gather.6.cloned.1.call-update) | async-done | bytes 2097168 | tf_op jit(solution)/shard_map/all_gather | solution.py:90
  224.2 16.3 %fusion.56 = f32[512,256]{1,0:T(8,128)} fusion(f32[512,256]{1,0:T(8,128)} %fusion.91, bf16[2048,256]{1,0:T(8,128)(2,1)S(1)} %copy-done, bf16[64,2048]{1,0:T(8,128)(2,1)S(1)} %copy-done.6, f32[2048]{0:T(1024)S(1)} %copy-done.10, bf16[64,1536]{1,0:T(8,128)(2,1)S(1)} %copy-done.3), kind=kOutput, calls=%fused_computation.74 | convolution fusion | flops 674365440 | bytes 2433024 | tf_op jit(solution)/shard_map/dot_general | solution.py:86
  240.5 13.5 %reduce-scatter.7.cloned.1.call-done = f32[256,256]{1,0:T(8,128)} async-done(((f32[512,256]{1,0:T(8,128)}), f32[256,256]{1,0:T(8,128)}) %reduce-scatter.7.cloned.1.call-update) | async-done | bytes 262160 | tf_op jit(solution)/shard_map/reduce_scatter | solution.py:93
  255.8 5.6 %all-to-all-start.1 = ((f32[256,16,16]{0,2,1:T(8,128)}), f32[256,16,16]{0,2,1:T(8,128)S(1)}, u32[]{:S(2)}, u32[]{:S(2)}) async-start(f32[256,16,16]{0,2,1:T(8,128)} %bitcast.15), calls=%async_computation.3 | async-start | bytes 524288 | tf_op jit(solution)/shard_map/all_to_all | solution.py:94
  261.6 9.9 %all-to-all-done.1 = f32[256,16,16]{0,2,1:T(8,128)S(1)} async-done(((f32[256,16,16]{0,2,1:T(8,128)}), f32[256,16,16]{0,2,1:T(8,128)S(1)}, u32[]{:S(2)}, u32[]{:S(2)}) %all-to-all-start.1) | async-done | bytes 262176 | tf_op jit(solution)/shard_map/all_to_all | solution.py:94
  271.5 30.5 %fusion.42 = f32[4096,16]{0,1:T(8,128)S(1)} fusion(f32[4096,16]{0,1:T(8,128)S(1)} %bitcast.132, s32[4096]{0:T(1024)S(1)} %bitcast.139, f32[4096,16]{0,1:T(8,128)S(1)} %copy-done.8, f32[4096,16]{0,1:T(8,128)S(1)} %get-tuple-element.129, f32[4096]{0:T(1024)S(1)} %copy-done.9), kind=kOutput, calls=%fused_computation.56 | convolution fusion | flops 3238264832 | bytes 1081344 | tf_op jit(solution)/shard_map/dot_general | solution.py:100
  302.0 23.1 %fusion.86 = (bf16[4096,16]{0,1:T(8,128)(2,1)}, f32[4096,16]{0,1:T(8,128)S(1)}, f32[4096,16]{0,1:T(8,128)S(1)}) fusion(f32[4096,16]{0,1:T(8,128)} %copy-done.11, f32[4096,16]{0,1:T(8,128)S(1)} %fusion.42, s32[4096]{0:T(1024)S(1)} %bitcast.140, f32[4096,16]{0,1:T(8,128)S(1)} %copy-done.12), kind=kOutput, calls=%fused_computation.112 | convolution fusion | flops 3238330368 | bytes 1458176 | tf_op jit(solution)/shard_map/dot_general | solution.py:101
  327.7 8.5 %while.32 = (s32[]{:T(128)}, bf16[2,256,4096]{2,1,0:T(8,128)(2,1)}, bf16[2,64,256]{2,1,0:T(8,128)(2,1)S(1)}, f32[4096]{0:T(1024)S(1)}, bf16[64,4096]{1,0:T(8,128)(2,1)S(1)}, /*index=5*/s32[]{:T(128)}) while((s32[]{:T(128)}, bf16[2,256,4096]{2,1,0:T(8,128)(2,1)}, bf16[2,64,256]{2,1,0:T(8,128)(2,1)S(1)}, f32[4096]{0:T(1024)S(1)}, ...), condition=%wide.region_12.13_spmd, body=%wide.region_10.12_spmd.sunk | while | flops 143703808 | bytes 2706513 | solution.py:81
  336.2 27.8 %all-gather.8.cloned.1.call-done = bf16[4096,256]{0,1:T(8,128)(2,1)} async-done(((bf16[4096,16]{0,1:T(8,128)(2,1)}), bf16[4096,256]{0,1:T(8,128)(2,1)}) %all-gather.8.cloned.1.call-update) | async-done | bytes 2097168 | tf_op jit(solution)/shard_map/all_gather | solution.py:90
  368.1 15.2 %fusion.55 = f32[512,256]{1,0:T(8,128)} fusion(f32[512,256]{1,0:T(8,128)S(1)} %fusion.92, bf16[2048,256]{1,0:T(8,128)(2,1)S(1)} %copy-done, bf16[64,2048]{1,0:T(8,128)(2,1)S(1)} %copy-done.6, f32[2048]{0:T(1024)S(1)} %copy-done.10, bf16[64,1536]{1,0:T(8,128)(2,1)S(1)} %copy-done.3), kind=kOutput, calls=%fused_computation.73 | convolution fusion | flops 674365440 | bytes 2433024 | tf_op jit(solution)/shard_map/dot_general | solution.py:86
  383.5 57.3 %multiply_convert_fusion.3.clone.4 = bf16[2048,2048]{1,0:T(8,128)(2,1)S(1)} fusion(bf16[64,2048]{1,0:T(8,128)(2,1)S(1)} %copy-done.6, bf16[64,2048]{1,0:T(8,128)(2,1)S(1)} %copy-done.7, f32[2048]{0:T(1024)S(1)} %copy-done.10), kind=kOutput, calls=%fused_computation.53.clone.clone.clone.1 | convolution fusion | flops 549453824 | bytes 8921088 | tf_op jit(solution)/shard_map/dot_general | solution.py:19
  450.4 25.2 %reduce-scatter.11.cloned.1.call-done = f32[128,2048]{0,1:T(8,128)} async-done(((f32[256,2048]{0,1:T(8,128)}), f32[128,2048]{0,1:T(8,128)}) %reduce-scatter.11.cloned.1.call-update) | async-done | bytes 1048592 | tf_op jit(solution)/shard_map/reduce_scatter | solution.py:63
  478.1 30.4 %fusion.43 = f32[4096,16]{0,1:T(8,128)S(1)} fusion(f32[4096,16]{0,1:T(8,128)S(1)} %bitcast.133, s32[4096]{0:T(1024)S(1)} %bitcast.137, f32[4096,16]{0,1:T(8,128)S(1)} %copy-done.8, f32[4096,16]{0,1:T(8,128)S(1)} %get-tuple-element.127, f32[4096]{0:T(1024)S(1)} %copy-done.9), kind=kOutput, calls=%fused_computation.57 | convolution fusion | flops 3238264832 | bytes 1081344 | tf_op jit(solution)/shard_map/dot_general | solution.py:100
  508.5 22.3 %fusion.89 = (f32[4096,16]{0,1:T(8,128)}, f32[4096,16]{0,1:T(8,128)}) fusion(f32[4096,16]{0,1:T(8,128)S(1)} %get-tuple-element.127, f32[4096,16]{0,1:T(8,128)S(1)} %fusion.43, s32[4096]{0:T(1024)S(1)} %bitcast.138, f32[4096,16]{0,1:T(8,128)S(1)} %get-tuple-element.134), kind=kOutput, calls=%fused_computation.115 | convolution fusion | flops 3238264832 | bytes 1327104 | tf_op jit(solution)/shard_map/dot_general | solution.py:101
  (87 shorter events, 70.6 us)
Async XLA Ops:
  8.0 59.3 %copy-start = (bf16[2048,256]{1,0:T(8,128)(2,1)S(1)}, bf16[2048,256]{1,0:T(8,128)(2,1)}, u32[]{:S(2)}) copy-start(bf16[2048,256]{1,0:T(8,128)(2,1)} %param.23) | copy-start | bytes 3145732
  8.0 32.2 %all-reduce.2.cloned.1.call-start = ((), (), s32[]{:S(2)}) async-start(), calls=%async_computation.7 | async-start | bytes 393216 | tf_op jit(solution)/shard_map/psum | solution.py:61
  8.9 6.1 %copy-start.2 = (f32[4096,16]{0,1:T(8,128)S(1)}, f32[4096,16]{0,1:T(8,128)}, u32[]{:S(2)}) copy-start(f32[4096,16]{0,1:T(8,128)} %param.19) | copy-start | bytes 786436
  8.9 6.9 %copy-start.1 = (bf16[64,4096]{1,0:T(8,128)(2,1)S(1)}, bf16[64,4096]{1,0:T(8,128)(2,1)}, u32[]{:S(2)}) copy-start(bf16[64,4096]{1,0:T(8,128)(2,1)} %param.16) | copy-start | bytes 1572868
  14.9 47.4 %all-gather.4.cloned.1.call-start = ((), (), s32[]{:S(2)}) async-start(), calls=%async_computation.8 | async-start | bytes 2228224 | tf_op jit(solution)/shard_map/all_gather | solution.py:90
  15.7 94.5 %reduce-scatter.5.cloned.1.call-start = ((), (), s32[]{:S(2)}) async-start(), calls=%async_computation.9 | async-start | bytes 786432 | tf_op jit(solution)/shard_map/reduce_scatter | solution.py:93
  52.0 15.3 %copy-start.3 = (bf16[64,1536]{1,0:T(8,128)(2,1)S(1)}, bf16[64,1536]{1,0:T(8,128)(2,1)}, u32[]{:S(2)}) copy-start(bf16[64,1536]{1,0:T(8,128)(2,1)} %all-reduce.2.cloned.1.call-done) | copy-start | bytes 589828
  52.0 15.3 %copy-start.6 = (bf16[64,2048]{1,0:T(8,128)(2,1)S(1)}, bf16[64,2048]{1,0:T(8,128)(2,1)}, u32[]{:S(2)}) copy-start(bf16[64,2048]{1,0:T(8,128)(2,1)} %param.21) | copy-start | bytes 786436
  52.0 15.3 %copy-start.10 = (f32[2048]{0:T(1024)S(1)}, f32[2048]{0:T(1024)}, u32[]{:S(2)}) copy-start(f32[2048]{0:T(1024)} %param.22) | copy-start | bytes 24580
  67.3 50.4 %copy-start.4 = (s32[3,8192]{1,0:T(4,128)S(1)}, s32[3,8192]{1,0:T(4,128)}, u32[]{:S(2)}) copy-start(s32[3,8192]{1,0:T(4,128)} %param.25) | copy-start | bytes 294916
  67.3 60.4 %copy-start.8 = (f32[4096,16]{0,1:T(8,128)S(1)}, f32[4096,16]{0,1:T(8,128)}, u32[]{:S(2)}) copy-start(f32[4096,16]{0,1:T(8,128)} %param.18) | copy-start | bytes 786436
  67.3 60.4 %copy-start.9 = (f32[4096]{0:T(1024)S(1)}, f32[4096]{0:T(1024)}, u32[]{:S(2)}) copy-start(f32[4096]{0:T(1024)} %param.17) | copy-start | bytes 49156
  112.0 15.6 %all-to-all-start = ((f32[256,16,16]{0,2,1:T(8,128)}), f32[256,16,16]{0,2,1:T(8,128)S(1)}, u32[]{:S(2)}, u32[]{:S(2)}) async-start(f32[256,16,16]{0,2,1:T(8,128)} %bitcast.10), calls=%async_computation.1 | async-start | bytes 524288 | tf_op jit(solution)/shard_map/all_to_all | solution.py:94
  117.6 101.7 %all-gather.6.cloned.1.call-start = ((), (), s32[]{:S(2)}) async-start(), calls=%async_computation.10 | async-start | bytes 2228224 | tf_op jit(solution)/shard_map/all_gather | solution.py:90
  127.7 30.5 %copy-start.5 = (f32[4096,16]{0,1:T(8,128)S(1)}, f32[4096,16]{0,1:T(8,128)}, u32[]{:S(2)}) copy-start(f32[4096,16]{0,1:T(8,128)} %param.20) | copy-start | bytes 786436
  180.5 91.0 %copy-start.11 = (f32[4096,16]{0,1:T(8,128)}, f32[4096,16]{0,1:T(8,128)S(1)}, u32[]{:S(2)}) copy-start(f32[4096,16]{0,1:T(8,128)S(1)} %get-tuple-element.129) | copy-start | bytes 786436
  180.5 73.6 %reduce-scatter.7.cloned.1.call-start = ((), (), s32[]{:S(2)}) async-start(), calls=%async_computation.11 | async-start | bytes 786432 | tf_op jit(solution)/shard_map/reduce_scatter | solution.py:93
  255.8 15.6 %all-to-all-start.1 = ((f32[256,16,16]{0,2,1:T(8,128)}), f32[256,16,16]{0,2,1:T(8,128)S(1)}, u32[]{:S(2)}, u32[]{:S(2)}) async-start(f32[256,16,16]{0,2,1:T(8,128)} %bitcast.15), calls=%async_computation.3 | async-start | bytes 524288 | tf_op jit(solution)/shard_map/all_to_all | solution.py:94
  261.5 102.5 %all-gather.8.cloned.1.call-start = ((), (), s32[]{:S(2)}) async-start(), calls=%async_computation.12 | async-start | bytes 2228224 | tf_op jit(solution)/shard_map/all_gather | solution.py:90
  271.5 30.5 %copy-start.12 = (f32[4096,16]{0,1:T(8,128)S(1)}, f32[4096,16]{0,1:T(8,128)}, u32[]{:S(2)}) copy-start(f32[4096,16]{0,1:T(8,128)} %get-tuple-element.133) | copy-start | bytes 786436
  325.2 119.6 %reduce-scatter.9.cloned.1.call-start = ((), (), s32[]{:S(2)}) async-start(), calls=%async_computation.13 | async-start | bytes 786432 | tf_op jit(solution)/shard_map/reduce_scatter | solution.py:93
  368.1 15.3 %copy-start.7 = (bf16[64,2048]{1,0:T(8,128)(2,1)S(1)}, bf16[64,2048]{1,0:T(8,128)(2,1)}, u32[]{:S(2)}) copy-start(bf16[64,2048]{1,0:T(8,128)(2,1)} %param.24) | copy-start | bytes 786436
  383.4 92.1 %reduce-scatter.11.cloned.1.call-start = ((), (), s32[]{:S(2)}) async-start(), calls=%async_computation.14 | async-start | bytes 3145728 | tf_op jit(solution)/shard_map/reduce_scatter | solution.py:63
  446.5 31.5 %all-to-all-start.2 = ((f32[256,16,16]{0,2,1:T(8,128)}), f32[256,16,16]{0,2,1:T(8,128)S(1)}, u32[]{:S(2)}, u32[]{:S(2)}) async-start(f32[256,16,16]{0,2,1:T(8,128)} %bitcast.20), calls=%async_computation.5 | async-start | bytes 524288 | tf_op jit(solution)/shard_map/all_to_all | solution.py:94
Sparse Core Ops, SparseCore 0:
  15.1 25.1 all-reduce.1
  96.8 13.3 reduce-scatter.4
  240.7 13.3 reduce-scatter.6
  383.5 13.3 reduce-scatter.8
  444.8 30.6 reduce-scatter.10
Sparse Core Ops, SparseCore 1:
  18.2 44.1 all-gather.3
  180.6 38.7 all-gather.5
  325.3 38.7 all-gather.7
where the time goes:
time: 539 us; the launch traced here: 538 us
  matrix products  325 us (60%)
  waiting for transfers between devices  162 us (30%)
  local copies, waits for them, and re-layouts  16.7 us (3%)
  between operations  16.1 us (3%)
  starting transfers between devices  15.3 us (3%)
    dot_general x3, matrix products, shards(): row_terms = arrived + jnp.dot(owner_map, point_terms, precision=HIGH)  91.4 us
    dot_general x3, matrix products, shards(): lax.dot_general(owner_map, row_terms, (((0,), (0,)), ((), ())), precision...  67.8 us
    all_gather x3, waiting for transfers between devices, shards(): coeffs = lax.all_gather(coeffs, 'row', axis=1, tiled=True)  65.8 us
    dot_general x3, matrix products, shards(): lax.dot_general(phi_batch, path_weights, (((0,), (0,)), ((), ())), prefer...  60.9 us
    dot_general x1, matrix products, features(): lax.dot_general(frequencies, points, (((0,), (0,)), ((), ())), preferred_...  57.3 us
    reduce_scatter x3, waiting for transfers between devices, shards(): lax.psum_scatter(partial_sum, 'col', scatter_dimension=0, tiled=True)  27 us
    reduce_scatter x1, waiting for transfers between devices, shards(): lax.psum_scatter(lax.dot_general(path_weights, phi_window, (((0,), (0,)),...  25.2 us
    psum x1, waiting for transfers between devices, shards(): batch_points = lax.psum(picked.astype(jnp.bfloat16), 'col')  24.3 us
  transfers between devices with their start and end apart: 11, of which 9 were waited for; matrix products, arithmetic and copies ran while one was open for 18% of the time, Pallas kernels for 0%

commit v1 on v0

v1 whole, which is shorter than its diff:
```python
import functools

import jax
import jax.numpy as jnp
import numpy as np
from jax import lax
from jax.experimental import pallas as pl
from jax.experimental.pallas import tpu as pltpu
from jax.sharding import PartitionSpec as P

SQRT_THREE = 1.7320508075688772
LENGTH = 1.15
NOISE_VAR = 0.25
MOMENTUM = 0.9
STEP_SIZE = 0.5


def sine_coeffs(scale):
    nodes = 5
    k = np.arange(nodes)
    v = (np.cos((2 * k + 1) * np.pi / (2 * nodes)) + 1) / 2 / 16
    z = np.sqrt(v)
    q = np.sin(2 * np.pi * z) / z
    return [float(c * scale) for c in np.linalg.solve(np.vander(v, nodes, increasing=True), q)]


def scaled_cos(turns, coeffs):
    z = 0.25 - jnp.abs(turns - jnp.round(turns))
    v = z * z
    q = coeffs[-1]
    for c in coeffs[-2::-1]:
        q = q * v + c
    return q * z


def prior_kernel(coeffs, tile_f, freq_ref, phase_ref, weight_ref, point_ref, out_ref):
    feat = freq_ref.shape[0]
    points = point_ref[...]

    def body(i, acc):
        rows = pl.ds(pl.multiple_of(i * tile_f, tile_f), tile_f)
        arg = jnp.dot(freq_ref[rows, :], points, preferred_element_type=jnp.float32)
        turns = (arg + phase_ref[rows, :]) * (0.5 / np.pi)
        phi = scaled_cos(turns, coeffs).astype(jnp.bfloat16)
        return acc + lax.dot_general(
            weight_ref[rows, :], phi, (((0,), (0,)), ((), ())), preferred_element_type=jnp.float32
        )

    out_ref[...] = lax.fori_loop(0, feat // tile_f, body, jnp.zeros(out_ref.shape, jnp.float32))


def prior_sums(freq_t, phase_col, weights, points, total_feat):
    feat, d_in = freq_t.shape
    paths = weights.shape[1]
    n = points.shape[1]
    tile_n = min(512, n)
    coeffs = sine_coeffs((2.0 / total_feat) ** 0.5)
    return pl.pallas_call(
        functools.partial(prior_kernel, coeffs, min(256, feat)),
        grid=(n // tile_n,),
        in_specs=[
            pl.BlockSpec((feat, d_in), lambda i: (0, 0)),
            pl.BlockSpec((feat, 1), lambda i: (0, 0)),
            pl.BlockSpec((feat, paths), lambda i: (0, 0)),
            pl.BlockSpec((d_in, tile_n), lambda i: (0, i)),
        ],
        out_specs=pl.BlockSpec((paths, tile_n), lambda i: (0, i)),
        out_shape=jax.ShapeDtypeStruct((paths, n), jnp.float32),
        cost_estimate=pl.CostEstimate(
            flops=2 * feat * n * (paths + d_in), bytes_accessed=4 * paths * n, transcendentals=feat * n
        ),
    )(freq_t, phase_col, weights, points)


def matern(points, train):
    inner = lax.dot_general(
        train, points, (((0,), (0,)), ((), ())), preferred_element_type=jnp.float32
    )
    point_norm = jnp.sum(jnp.square(points.astype(jnp.float32)), axis=0)
    train_norm = jnp.sum(jnp.square(train.astype(jnp.float32)), axis=0)
    dist_sq = jnp.maximum(train_norm[:, None] + point_norm[None, :] - 2.0 * inner, 0.0)
    scaled = SQRT_THREE / LENGTH * jnp.sqrt(dist_sq)
    return ((1.0 + scaled) * jnp.exp(-scaled)).astype(jnp.bfloat16)


def point_counts(index, start, count):
    lanes = 128
    local = index - start
    high = (local // lanes)[:, None, :] == lax.broadcasted_iota(
        jnp.int32, (1, count // lanes, 1), 1
    )
    low = (local % lanes)[:, None, :] == lax.broadcasted_iota(jnp.int32, (1, lanes, 1), 1)
    tables = lax.dot_general(
        high.astype(jnp.bfloat16),
        low.astype(jnp.bfloat16),
        (((2,), (2,)), ((0,), (0,))),
        preferred_element_type=jnp.float32,
    )
    return tables.reshape(index.shape[0], count)


def shards(
    x_train,
    targets,
    noise_draws,
    alpha_init,
    velocity_init,
    frequencies,
    phases,
    path_weights,
    x_window,
    batch_index,
):
    row_count = lax.axis_size("row")
    col_count = lax.axis_size("col")
    row_id = lax.axis_index("row")
    col_id = lax.axis_index("col")
    train_cols = x_train.shape[1]
    own = train_cols // row_count
    steps = batch_index.shape[0]
    total_feat = frequencies.shape[1] * col_count

    mine = lax.dynamic_slice_in_dim(x_train, row_id * own, own, 1)
    points = lax.all_gather(mine, "col", axis=1, tiled=True)
    freq_t = frequencies.T
    phase_col = phases[:, None]
    kernel_tile = matern(points, x_train)
    prior_rows = prior_sums(freq_t, phase_col, path_weights, points, total_feat)
    window = prior_sums(freq_t, phase_col, path_weights, x_window, total_feat)
    prior_window = lax.psum_scatter(window, "col", scatter_dimension=0, tiled=True)

    counts = point_counts(batch_index, col_id * train_cols, train_cols)
    base = (noise_draws - targets[:, None]).T
    dual, velocity = alpha_init.T, velocity_init.T
    for step in range(steps):
        coeffs = lax.all_gather(dual.astype(jnp.bfloat16), "row", axis=0, tiled=True)
        sums = jnp.dot(coeffs, kernel_tile, preferred_element_type=jnp.float32) + prior_rows
        mine_sums = lax.psum_scatter(sums, "col", scatter_dimension=1, tiled=True)
        arrived = lax.all_to_all(mine_sums, "row", split_axis=0, concat_axis=1, tiled=True)
        gradient = counts[step][None, :] * (arrived + NOISE_VAR * dual + base)
        velocity = MOMENTUM * velocity - STEP_SIZE * gradient
        dual = dual + velocity
    return (dual.T, velocity.T, prior_window)


def solution(mesh):
    placed = (
        P(None, "col"),
        P("col"),
        P("col", "row"),
        P("col", "row"),
        P("col", "row"),
        P(None, "col"),
        P("col"),
        P("col", None),
        P(None, "row"),
        P(),
    )
    return jax.shard_map(
        shards,
        mesh=mesh,
        in_specs=placed,
        out_specs=(P("col", "row"), P("col", "row"), P("col", "row")),
        check_vma=False,
    )
```

time: 539 us -> 270 us (0.50)
  matrix products: 325 us -> 24.8 us
  blocking collectives: 0 us -> 34.8 us
  Pallas kernels: 0 us -> 32.6 us
  waiting for transfers between devices: 162 us -> 147 us
  local copies, waits for them, and re-layouts: 16.7 us -> 4.85 us
  starting transfers between devices: 15.3 us -> 5.92 us
    dot_general x21 -> x5, matrix products: 325 us -> 24.8 us  [the longest x3 14.7 us: shards(): jnp.dot(coeffs, kernel_tile, preferred_element_type=jnp.float32)]
    pallas_call x0 -> x2, Pallas kernels: none -> 32.6 us  [prior_sums(): pl.pallas_call(functools.partial(prior_kernel, coeffs, min(256, feat)), g...]
    all_gather x3, waiting for transfers between devices: 65.8 us -> 96.5 us  [shards(): lax.all_gather(dual.astype(jnp.bfloat16), 'row', axis=0, tiled=True)]
    all_to_all x0 -> x2, blocking collectives: none -> 29.1 us  [shards(): lax.all_to_all(mine_sums, 'row', split_axis=0, concat_axis=1, tiled=True)]
    psum x1 -> x0, waiting for transfers between devices: 24.3 us -> none  [shards(): batch_points = lax.psum(picked.astype(jnp.bfloat16), 'col')]
    all_to_all x3 -> x1, waiting for transfers between devices: 19.5 us -> 7.27 us  [shards(): lax.all_to_all(mine_sums, 'row', split_axis=0, concat_axis=1, tiled=True)]
    all_to_all x3 -> x1, starting transfers between devices: 15 us -> 5.63 us  [shards(): lax.all_to_all(mine_sums, 'row', split_axis=0, concat_axis=1, tiled=True)]
    reduce_scatter x4, waiting for transfers between devices: 52.2 us -> 43.2 us  [the longest x3 27 us: shards(): mine_sums = lax.psum_scatter(sums, 'col', scatter_dimension=1, tiled=True)]
  transfers between devices with their start and end apart: 11 -> 8, of which waited for: 9 -> 7; matrix products, arithmetic and copies ran while one was open for 18% -> 6% of each run, Pallas kernels for 0% -> 12%
where the time goes in v1:
time: 270 us
  waiting for transfers between devices  147 us (54%)
  blocking collectives  34.8 us (13%)
  Pallas kernels  32.6 us (12%)
  matrix products  24.8 us (9%)
  between operations  14.3 us (5%)
  starting transfers between devices  5.92 us (2%)
  other arithmetic  5.47 us (2%)
  local copies, waits for them, and re-layouts  4.85 us (2%)
    all_gather x3, waiting for transfers between devices, shards(): lax.all_gather(dual.astype(jnp.bfloat16), 'row', axis=0, tiled=True)  96.5 us
    pallas_call x2, Pallas kernels, prior_sums(): pl.pallas_call(functools.partial(prior_kernel, coeffs, min(256, feat)), g...  32.6 us
    all_to_all x2, blocking collectives, shards(): lax.all_to_all(mine_sums, 'row', split_axis=0, concat_axis=1, tiled=True)  29.1 us
    reduce_scatter x3, waiting for transfers between devices, shards(): mine_sums = lax.psum_scatter(sums, 'col', scatter_dimension=1, tiled=True)  27 us
    reduce_scatter x1, waiting for transfers between devices, shards(): lax.psum_scatter(window, 'col', scatter_dimension=0, tiled=True)  16.2 us
    dot_general x3, matrix products, shards(): jnp.dot(coeffs, kernel_tile, preferred_element_type=jnp.float32)  14.7 us
    dot_general x1, matrix products, matern(): lax.dot_general(train, points, (((0,), (0,)), ((), ())), preferred_elemen...  7.62 us
    all_to_all x1, waiting for transfers between devices, shards(): lax.all_to_all(mine_sums, 'row', split_axis=0, concat_axis=1, tiled=True)  7.27 us
  transfers between devices with their start and end apart: 8, of which 7 were waited for; matrix products, arithmetic and copies ran while one was open for 6% of the time, Pallas kernels for 12%

profile of v1, /device:TPU:0, one launch (start us, length us, event | category | flops | bytes accessed | tf_op | source)
XLA Modules:
  0.0 269.8 jit_solution(2077983342167396467)
XLA Ops:
  7.2 1.7 bitcast_convert_fusion
  9.0 2.0 copy.19
  10.9 2.0 copy.20.phase_ref
  13.7 5.6 %all_gather.12.point_ref = bf16[64,512]{1,0:T(8,128)(2,1)} all-gather(bf16[64,256]{1,0:T(8,128)(2,1)S(1)} %constant_dynamic-slice_fusion), channel_id=1, replica_groups=mesh['row'=16,'col'=2] {'col'}, dimensions={1}, use_global_device_ids=true | all-gather | bytes 98304 | tf_op jit(solution)/shard_map/all_gather | solution.py:124
  19.4 8.0 %shard_map.121 = f32[256,512]{1,0:T(8,128)} custom-call(bf16[2048,64]{1,0:T(8,128)(2,1)} %bitcast.116, f32[2048,1]{1,0:T(8,128)} %copy.20.phase_ref, bf16[2048,256]{1,0:T(8,128)(2,1)} %weight_ref.3, bf16[64,512]{1,0:T(8,128)(2,1)} %all_gather.12.point_ref), custom_call_target="tpu_custom_call" | custom-call | flops 671088640 | bytes 524288 | tf_op jit(solution)/shard_map/pallas_call | solution.py:58
  27.4 0.9 multiply_reduce_fusion.1
  28.4 7.6 %multiply_convert_fusion = bf16[4096,512]{0,1:T(8,128)(2,1)} fusion(bf16[64,512]{1,0:T(8,128)(2,1)} %all_gather.12.point_ref, bf16[64,4096]{1,0:T(8,128)(2,1)S(1)} %copy-done.3, f32[512]{0:T(512)S(1)} %multiply_reduce_fusion.1, f32[4096]{0:T(1024)S(1)} %multiply_reduce_fusion), kind=kOutput, calls=%fused_computation.6 | convolution fusion | flops 287309824 | bytes 4802560 | tf_op jit(solution)/shard_map/dot_general | solution.py:76
  36.0 18.9 %all-gather.4.cloned.1.call-done = bf16[256,4096]{1,0:T(8,128)(2,1)} async-done(((bf16[16,4096]{1,0:T(8,128)(2,1)}), bf16[256,4096]{1,0:T(8,128)(2,1)}) %all-gather.4.cloned.1.call-update) | async-done | bytes 2097168 | tf_op jit(solution)/shard_map/all_gather | solution.py:136
  54.9 4.9 %fusion.6 = f32[256,512]{1,0:T(8,128)} fusion(f32[256,512]{1,0:T(8,128)S(1)} %copy-done.4, bf16[4096,512]{0,1:T(8,128)(2,1)} %multiply_convert_fusion, bf16[256,4096]{1,0:T(8,128)(2,1)} %all-gather.4.cloned.1.call-done), kind=kOutput, calls=%fused_computation.11 | convolution fusion | flops 1073872896 | bytes 7340032 | tf_op jit(solution)/shard_map/dot_general | solution.py:137
  59.9 13.5 %reduce-scatter.5.cloned.1.call-done = f32[256,256]{1,0:T(8,128)} async-done(((f32[256,512]{1,0:T(8,128)}), f32[256,256]{1,0:T(8,128)}) %reduce-scatter.5.cloned.1.call-update) | async-done | bytes 262160 | tf_op jit(solution)/shard_map/reduce_scatter | solution.py:138
  73.4 5.6 %all-to-all-start = ((f32[16,16,256]{2,1,0:T(8,128)}), f32[16,16,256]{2,1,0:T(8,128)S(1)}, u32[]{:S(2)}, u32[]{:S(2)}) async-start(f32[16,16,256]{2,1,0:T(8,128)} %bitcast.123), calls=%async_computation.1 | async-start | bytes 524288 | tf_op jit(solution)/shard_map/all_to_all | solution.py:139
  79.4 2.4 fusion
  81.8 7.3 %all-to-all-done = f32[16,16,256]{2,1,0:T(8,128)S(1)} async-done(((f32[16,16,256]{2,1,0:T(8,128)}), f32[16,16,256]{2,1,0:T(8,128)S(1)}, u32[]{:S(2)}, u32[]{:S(2)}) %all-to-all-start) | async-done | bytes 262176 | tf_op jit(solution)/shard_map/all_to_all | solution.py:139
  90.0 38.8 %all-gather.6.cloned.1.call-done = bf16[256,4096]{1,0:T(8,128)(2,1)} async-done(((bf16[16,4096]{1,0:T(8,128)(2,1)}), bf16[256,4096]{1,0:T(8,128)(2,1)}) %all-gather.6.cloned.1.call-update) | async-done | bytes 2097168 | tf_op jit(solution)/shard_map/all_gather | solution.py:136
  128.8 4.9 %convolution_add_fusion.1 = f32[256,512]{1,0:T(8,128)} fusion(f32[256,512]{1,0:T(8,128)S(1)} %copy-done.4, bf16[256,4096]{1,0:T(8,128)(2,1)} %all-gather.6.cloned.1.call-done, bf16[4096,512]{0,1:T(8,128)(2,1)} %multiply_convert_fusion), kind=kOutput, calls=%fused_computation.13 | convolution fusion | flops 1073872896 | bytes 7340032 | tf_op jit(solution)/shard_map/dot_general | solution.py:137
  133.8 13.5 %reduce-scatter.7.cloned.1.call-done = f32[256,256]{1,0:T(8,128)} async-done(((f32[256,512]{1,0:T(8,128)}), f32[256,256]{1,0:T(8,128)}) %reduce-scatter.7.cloned.1.call-update) | async-done | bytes 262160 | tf_op jit(solution)/shard_map/reduce_scatter | solution.py:138
  147.2 15.6 %all_to_all.57 = f32[16,16,256]{2,1,0:T(8,128)S(1)} all-to-all(f32[16,16,256]{2,1,0:T(8,128)} %bitcast.125), channel_id=1, replica_groups=mesh['row'=16,'col'=2] {'row'}, dimensions={0} | all-to-all | bytes 524288 | tf_op jit(solution)/shard_map/all_to_all | solution.py:139
  162.9 0.8 fusion.21
  163.8 38.8 %all-gather.8.cloned.1.call-done = bf16[256,4096]{1,0:T(8,128)(2,1)} async-done(((bf16[16,4096]{1,0:T(8,128)(2,1)}), bf16[256,4096]{1,0:T(8,128)(2,1)}) %all-gather.8.cloned.1.call-update) | async-done | bytes 2097168 | tf_op jit(solution)/shard_map/all_gather | solution.py:136
  202.6 4.9 %convolution_add_fusion = f32[256,512]{1,0:T(8,128)} fusion(f32[256,512]{1,0:T(8,128)S(1)} %copy-done.4, bf16[256,4096]{1,0:T(8,128)(2,1)} %all-gather.8.cloned.1.call-done, bf16[4096,512]{0,1:T(8,128)(2,1)} %multiply_convert_fusion), kind=kOutput, calls=%fused_computation.12 | convolution fusion | flops 1073872896 | bytes 7340032 | tf_op jit(solution)/shard_map/dot_general | solution.py:137
  207.5 24.6 %shard_map.122 = f32[256,2048]{1,0:T(8,128)} custom-call(bf16[2048,64]{1,0:T(8,128)(2,1)} %bitcast.117, f32[2048,1]{1,0:T(8,128)} %copy.20.phase_ref, bf16[2048,256]{1,0:T(8,128)(2,1)} %weight_ref.3, bf16[64,2048]{1,0:T(8,128)(2,1)} %point_ref.1), custom_call_target="tpu_custom_call" | custom-call | flops 2684354560 | bytes 2097152 | tf_op jit(solution)/shard_map/pallas_call | solution.py:58
  232.2 13.5 %all_to_all.58 = f32[16,16,256]{2,1,0:T(8,128)S(1)} all-to-all(f32[16,16,256]{2,1,0:T(8,128)} %bitcast.124), channel_id=1, replica_groups=mesh['row'=16,'col'=2] {'row'}, dimensions={0} | all-to-all | bytes 524288 | tf_op jit(solution)/shard_map/all_to_all | solution.py:139
  245.7 1.0 add_bitcast_fusion
  246.7 16.2 %reduce-scatter.11.cloned.1.call-done = f32[128,2048]{1,0:T(8,128)} async-done(((f32[256,2048]{1,0:T(8,128)}), f32[128,2048]{1,0:T(8,128)}) %reduce-scatter.11.cloned.1.call-update) | async-done | bytes 1048592 | tf_op jit(solution)/shard_map/reduce_scatter | solution.py:130
  (37 shorter events, 2.4 us)
Async XLA Ops:
  7.2 21.1 %copy-start.3 = (bf16[64,4096]{1,0:T(8,128)(2,1)S(1)}, bf16[64,4096]{1,0:T(8,128)(2,1)}, u32[]{:S(2)}) copy-start(bf16[64,4096]{1,0:T(8,128)(2,1)} %param.10) | copy-start | bytes 1572868
  7.2 47.8 %all-gather.4.cloned.1.call-start = ((), (), s32[]{:S(2)}) async-start(), calls=%async_computation.7 | async-start | bytes 2228224 | tf_op jit(solution)/shard_map/all_gather | solution.py:136
  8.9 64.5 %reduce-scatter.5.cloned.1.call-start = ((), (), s32[]{:S(2)}) async-start(), calls=%async_computation.8 | async-start | bytes 786432 | tf_op jit(solution)/shard_map/reduce_scatter | solution.py:138
  28.4 26.5 %copy-start.4 = (f32[256,512]{1,0:T(8,128)S(1)}, f32[256,512]{1,0:T(8,128)}, u32[]{:S(2)}) copy-start(f32[256,512]{1,0:T(8,128)} %shard_map.121) | copy-start | bytes 1572868
  36.0 43.1 %copy-start.6 = (s32[3,8192]{1,0:T(4,128)S(1)}, s32[3,8192]{1,0:T(4,128)}, u32[]{:S(2)}) copy-start(s32[3,8192]{1,0:T(4,128)} %param.19) | copy-start | bytes 294916
  59.9 29.2 %copy-start = (f32[4096,16]{0,1:T(8,128)S(1)}, f32[4096,16]{0,1:T(8,128)}, u32[]{:S(2)}) copy-start(f32[4096,16]{0,1:T(8,128)} %param.13) | copy-start | bytes 786436
  59.9 29.2 %copy-start.1 = (f32[4096,16]{0,1:T(8,128)S(1)}, f32[4096,16]{0,1:T(8,128)}, u32[]{:S(2)}) copy-start(f32[4096,16]{0,1:T(8,128)} %param.12) | copy-start | bytes 786436
  59.9 29.2 %copy-start.2 = (f32[4096,16]{0,1:T(8,128)S(1)}, f32[4096,16]{0,1:T(8,128)}, u32[]{:S(2)}) copy-start(f32[4096,16]{0,1:T(8,128)} %param.14) | copy-start | bytes 786436
  59.9 29.2 %copy-start.5 = (f32[4096]{0:T(1024)S(1)}, f32[4096]{0:T(1024)}, u32[]{:S(2)}) copy-start(f32[4096]{0:T(1024)} %param.11) | copy-start | bytes 49156
  73.4 15.7 %all-to-all-start = ((f32[16,16,256]{2,1,0:T(8,128)}), f32[16,16,256]{2,1,0:T(8,128)S(1)}, u32[]{:S(2)}, u32[]{:S(2)}) async-start(f32[16,16,256]{2,1,0:T(8,128)} %bitcast.123), calls=%async_computation.1 | async-start | bytes 524288 | tf_op jit(solution)/shard_map/all_to_all | solution.py:139
  79.1 49.7 %all-gather.6.cloned.1.call-start = ((), (), s32[]{:S(2)}) async-start(), calls=%async_computation.9 | async-start | bytes 2228224 | tf_op jit(solution)/shard_map/all_gather | solution.py:136
  89.9 57.3 %reduce-scatter.7.cloned.1.call-start = ((), (), s32[]{:S(2)}) async-start(), calls=%async_computation.10 | async-start | bytes 786432 | tf_op jit(solution)/shard_map/reduce_scatter | solution.py:138
  133.7 68.9 %all-gather.8.cloned.1.call-start = ((), (), s32[]{:S(2)}) async-start(), calls=%async_computation.11 | async-start | bytes 2228224 | tf_op jit(solution)/shard_map/all_gather | solution.py:136
  163.7 68.5 %reduce-scatter.9.cloned.1.call-start = ((), (), s32[]{:S(2)}) async-start(), calls=%async_computation.12 | async-start | bytes 786432 | tf_op jit(solution)/shard_map/reduce_scatter | solution.py:138
  207.5 55.5 %reduce-scatter.11.cloned.1.call-start = ((), (), s32[]{:S(2)}) async-start(), calls=%async_computation.13 | async-start | bytes 3145728 | tf_op jit(solution)/shard_map/reduce_scatter | solution.py:130
Sparse Core Ops, SparseCore 0:
  10.7 44.1 all-gather.3
  60.0 13.3 reduce-scatter.4
  90.0 38.6 all-gather.5
  133.8 13.3 reduce-scatter.6
  163.8 38.6 all-gather.7
  207.6 13.3 reduce-scatter.8
  232.3 30.6 reduce-scatter.10

commit v2 on v1

--- a/solution.py
+++ b/solution.py
@@ -143,7 +143,347 @@
     return (dual.T, velocity.T, prior_window)
 
 
+MESH = pl.DeviceIdType.MESH
+
+
+def fused_kernel(
+    scale_coeffs, steps, rows, x_ref, target_ref, noise_ref, alpha_in, velocity_in, freq_ref,
+    phase_ref, weight_ref, window_ref, count_ref, alpha_ref, velocity_ref, prior_ref,
+    gathered, tile, train_prior, points, points_t, base, outboxes, arrivals, last_outbox, last_arrived,
+    window_out, window_in,
+    ring_send, ring_recv, pair_send, pair_recv, sum_send, sum_recv, misc_send, misc_recv,
+):
+    div, rem = lax.div, lax.rem
+    row = lax.axis_index("row")
+    col = lax.axis_index("col")
+    peer = 1 - col
+    devices = rows * 2
+    flat = row * 2 + col
+    paths = weight_ref.shape[0]
+    share = paths // rows
+    train = x_ref.shape[1]
+    own = train // rows
+    feat = freq_ref.shape[1]
+    half = train // 2
+    chips = rows // 2
+    core = rem(row, 2)
+    chip = div(row, 2)
+    depth, side = div(chip, 2), rem(chip, 2)
+    place = depth * (1 - side) + (chips - 1 - depth) * side
+
+    def row_at(position, on_core):
+        p = rem(position + 2 * chips, chips)
+        back = div(p, chips // 2)
+        return ((1 - back) * 2 * p + back * (2 * (chips - 1 - p) + 1)) * 2 + on_core
+
+    def device(d):
+        other = rem(flat + d, devices)
+        return div(other, 2), rem(other, 2)
+
+    barrier = pltpu.get_barrier_semaphore()
+
+    def greet(d, carry):
+        pl.semaphore_signal(barrier, inc=1, device_id=device(d), device_id_type=MESH)
+        return carry
+
+    lax.fori_loop(1, devices, greet, 0)
+
+    def block(step, r, h):
+        return gathered.at[
+            step, pl.ds(pl.multiple_of(r * share, share), share), pl.ds(h * half, half)
+        ]
+
+    def whole_block(step, r):
+        return gathered.at[step, pl.ds(pl.multiple_of(r * share, share), share), :]
+
+    def ring_copy(step, way, k, h):
+        sign = 1 - 2 * way
+        ref = block(step, row_at(place - sign * k, core), h)
+        return pltpu.make_async_remote_copy(
+            src_ref=ref, dst_ref=ref,
+            send_sem=ring_send.at[step, way, k, h], recv_sem=ring_recv.at[step, way, k, h],
+            device_id=(row_at(place + sign, core), col), device_id_type=MESH,
+        )
+
+    def pair_copy(step, way, k, h):
+        sign = 1 - 2 * way
+        ref = block(step, row_at(place - sign * (k + 1), core), h)
+        return pltpu.make_async_remote_copy(
+            src_ref=ref, dst_ref=ref,
+            send_sem=pair_send.at[step, way, k, h], recv_sem=pair_recv.at[step, way, k, h],
+            device_id=(row + 1 - 2 * core, col), device_id_type=MESH,
+        )
+
+    def own_copy(step):
+        ref = whole_block(step, row)
+        return pltpu.make_async_remote_copy(
+            src_ref=ref, dst_ref=ref,
+            send_sem=misc_send.at[step], recv_sem=misc_recv.at[step],
+            device_id=(row + 1 - 2 * core, col), device_id_type=MESH,
+        )
+
+    last = chips // 2 - 1
+
+    def hops(action):
+        def event(e, carry):
+            k, h = div(e, 2), rem(e, 2)
+            for way in (0, 1):
+                @pl.when((k < last) | (h == way))
+                def _():
+                    action(way, k, h)
+            return carry
+
+        lax.fori_loop(0, 2 * (last + 1), event, 0)
+
+    def gather(step, compute):
+        gathered[step, pl.ds(pl.multiple_of(row * share, share), share), :] = alpha_ref[
+            ...
+        ].astype(jnp.bfloat16)
+        for h in (0, 1):
+            for way in (0, 1):
+                ring_copy(step, way, 0, h).start()
+        own_copy(step).start()
+
+        def event(e, carry):
+            compute(e)
+            k, h = div(e, 2), rem(e, 2)
+            for way in (0, 1):
+                @pl.when((k < last) | (h == way))
+                def _():
+                    ring_copy(step, way, k, h).wait_recv()
+
+                    @pl.when((k < last - 1) | ((k == last - 1) & (h == way)))
+                    def _():
+                        ring_copy(step, way, k + 1, h).start()
+
+                    pair_copy(step, way, k, h).start()
+            return carry
+
+        lax.fori_loop(0, 2 * (last + 1), event, 0)
+        own_copy(step).wait_recv()
+        hops(lambda way, k, h: pair_copy(step, way, k, h).wait_recv())
+
+    def boxes(step):
+        if step < steps - 1:
+            return outboxes.at[step], arrivals.at[step]
+        return last_outbox, last_arrived
+
+    def sum_copy(step, d):
+        r, c = device(d)
+        outbox, arrived = boxes(step)
+        return pltpu.make_async_remote_copy(
+            src_ref=outbox.at[
+                pl.ds(pl.multiple_of(r * share, share), share),
+                pl.ds(pl.multiple_of(c * own, own), own),
+            ],
+            dst_ref=arrived.at[col, :, pl.ds(pl.multiple_of(row * own, own), own)],
+            send_sem=sum_send.at[step, d], recv_sem=sum_recv.at[step, d],
+            device_id=(r, c), device_id_type=MESH,
+        )
+
+    def point_copy():
+        return pltpu.make_async_remote_copy(
+            src_ref=x_ref.at[:, pl.ds(pl.multiple_of(row * own, own), own)],
+            dst_ref=points.at[col],
+            send_sem=misc_send.at[steps], recv_sem=misc_recv.at[steps],
+            device_id=(row, peer), device_id_type=MESH,
+        )
+
+    def window_copy(part):
+        width = window_out.shape[2]
+        return pltpu.make_async_remote_copy(
+            src_ref=window_out.at[part], dst_ref=window_in.at[part],
+            send_sem=misc_send.at[steps + 1 + part], recv_sem=misc_recv.at[steps + 1 + part],
+            device_id=(row, peer), device_id_type=MESH,
+        )
+
+    alpha_ref[...] = alpha_in[...]
+    velocity_ref[...] = velocity_in[...]
+    base[...] = noise_ref[...] - target_ref[...]
+    pl.semaphore_wait(barrier, devices - 1)
+    point_copy().start()
+    points[col] = x_ref[:, pl.ds(pl.multiple_of(row * own, own), own)]
+    train_prior[...] = jnp.zeros_like(train_prior)
+    events = 2 * (last + 1)
+
+    def phi_block(pts_t, cols):
+        arg = jnp.dot(pts_t, freq_ref[:, cols], preferred_element_type=jnp.float32)
+        turns = (arg + phase_ref[:, cols]) * (0.5 / np.pi)
+        return scaled_cos(turns, scale_coeffs).astype(jnp.bfloat16)
+
+    def against(a, b):
+        return lax.dot_general(
+            a, b, (((1,), (1,)), ((), ())), preferred_element_type=jnp.float32
+        )
+
+    def train_work(e):
+        @pl.when(e == 0)
+        def _():
+            point_copy().wait_recv()
+            for c in (0, 1):
+                points_t[c * own : (c + 1) * own, :] = points[c].astype(jnp.float32).T
+
+        width = train // events
+        cols = pl.ds(pl.multiple_of(e * width, width), width)
+        trains = x_ref[:, cols]
+        train_norm = jnp.sum(jnp.square(trains.astype(jnp.float32)), axis=0, keepdims=True)
+        fwidth = feat // events
+        fcols = pl.ds(pl.multiple_of(e * fwidth, fwidth), fwidth)
+        group = 128
+
+        def rows_of(i, carry):
+            span = pl.ds(pl.multiple_of(i * group, group), group)
+            pts = points_t[span, :]
+            pts_norm = jnp.sum(jnp.square(pts), axis=1, keepdims=True)
+            pts = pts.astype(jnp.bfloat16)
+            inner = jnp.dot(pts, trains, preferred_element_type=jnp.float32)
+            dist_sq = jnp.maximum(pts_norm + train_norm - 2.0 * inner, 0.0)
+            scaled = SQRT_THREE / LENGTH * jnp.sqrt(dist_sq)
+            tile[span, cols] = ((1.0 + scaled) * jnp.exp(-scaled)).astype(jnp.bfloat16)
+            train_prior[:, span] += against(weight_ref[:, fcols], phi_block(pts, fcols))
+            return carry
+
+        lax.fori_loop(0, 2 * own // group, rows_of, 0)
+
+    tiles = 2 * events
+    wide = window_ref.shape[1] // tiles
+
+    def window_work(part):
+        def work(e):
+            span = pl.ds(pl.multiple_of((part * events + e) * wide, wide), wide)
+            pts = window_ref[:, span].astype(jnp.float32).T.astype(jnp.bfloat16)
+            fwidth = min(512, feat)
+
+            def feats(i, acc):
+                fcols = pl.ds(pl.multiple_of(i * fwidth, fwidth), fwidth)
+                return acc + against(weight_ref[:, fcols], phi_block(pts, fcols))
+
+            acc = lax.fori_loop(
+                0, feat // fwidth, feats, jnp.zeros((paths, wide), jnp.float32)
+            )
+            kept = paths // 2
+            mine = jnp.where(col == 0, acc[:kept], acc[kept:])
+            sent = jnp.where(col == 0, acc[kept:], acc[:kept])
+            prior_ref[:, span] = mine
+            window_out[part, :, pl.ds(pl.multiple_of(e * wide, wide), wide)] = sent.astype(
+                jnp.bfloat16
+            )
+
+        return work
+
+    for step in range(steps):
+        if step == 0:
+            gather(step, train_work)
+        elif step < 3:
+            gather(step, window_work(step - 1))
+            window_copy(step - 1).start()
+        else:
+            gather(step, lambda e: None)
+        outbox, arrived = boxes(step)
+        for c in (0, 1):
+            span = slice(c * own, (c + 1) * own)
+            sums = against(gathered[step], tile[span, :]) + train_prior[:, span]
+            outbox[:, span] = sums.astype(outbox.dtype)
+
+        def send(d, carry):
+            sum_copy(step, d).start()
+            return carry
+
+        lax.fori_loop(1, devices, send, 0)
+        arrived[col, :, pl.ds(pl.multiple_of(row * own, own), own)] = outbox[
+            pl.ds(pl.multiple_of(row * share, share), share),
+            pl.ds(pl.multiple_of(col * own, own), own),
+        ]
+
+        def receive(d, carry):
+            sum_copy(step, d).wait_recv()
+            return carry
+
+        lax.fori_loop(1, devices, receive, 0)
+        total = arrived[0].astype(jnp.float32) + arrived[1].astype(jnp.float32)
+        alpha = alpha_ref[...]
+        gradient = count_ref[step : step + 1, :] * (total + NOISE_VAR * alpha + base[...])
+        speed = MOMENTUM * velocity_ref[...] - STEP_SIZE * gradient
+        velocity_ref[...] = speed
+        alpha_ref[...] = alpha + speed
+
+    for part in (0, 1):
+        window_copy(part).wait()
+        width = window_out.shape[2]
+        span = slice(part * width, (part + 1) * width)
+        prior_ref[:, span] = prior_ref[:, span] + window_in[part].astype(jnp.float32)
+    point_copy().wait_send()
+    for step in range(steps):
+        own_copy(step).wait_send()
+        hops(lambda way, k, h: ring_copy(step, way, k, h).wait_send())
+        hops(lambda way, k, h: pair_copy(step, way, k, h).wait_send())
+
+        def drain(d, carry):
+            sum_copy(step, d).wait_send()
+            return carry
+
+        lax.fori_loop(1, devices, drain, 0)
+
+
+def fused_shards(
+    x_train, targets, noise_draws, alpha_init, velocity_init, frequencies, phases, path_weights,
+    x_window, batch_index,
+):
+    rows = lax.axis_size("row")
+    col_count = lax.axis_size("col")
+    train = x_train.shape[1]
+    steps = batch_index.shape[0]
+    paths = path_weights.shape[1]
+    share = paths // rows
+    own = train // rows
+    window = x_window.shape[1]
+    counts = point_counts(batch_index, lax.axis_index("col") * train, train)
+    coeffs = sine_coeffs((2.0 / (frequencies.shape[1] * col_count)) ** 0.5)
+    vmem = pl.BlockSpec(memory_space=pltpu.VMEM)
+    dma = pltpu.SemaphoreType.DMA
+    hop_shape = (steps, 2, rows // 4, 2)
+    alpha, velocity, prior = pl.pallas_call(
+        functools.partial(fused_kernel, coeffs, steps, rows),
+        in_specs=[vmem] * 10,
+        out_specs=[vmem] * 3,
+        out_shape=(
+            jax.ShapeDtypeStruct((share, train), jnp.float32),
+            jax.ShapeDtypeStruct((share, train), jnp.float32),
+            jax.ShapeDtypeStruct((paths // 2, window), jnp.float32),
+        ),
+        scratch_shapes=[
+            pltpu.VMEM((steps, paths, train), jnp.bfloat16),
+            pltpu.VMEM((2 * own, train), jnp.bfloat16),
+            pltpu.VMEM((paths, 2 * own), jnp.float32),
+            pltpu.VMEM((2, x_train.shape[0], own), jnp.bfloat16),
+            pltpu.VMEM((2 * own, x_train.shape[0]), jnp.float32),
+            pltpu.VMEM((share, train), jnp.float32),
+            pltpu.VMEM((steps - 1, paths, 2 * own), jnp.float32),
+            pltpu.VMEM((steps - 1, 2, share, train), jnp.float32),
+            pltpu.VMEM((paths, 2 * own), jnp.bfloat16),
+            pltpu.VMEM((2, share, train), jnp.bfloat16),
+            pltpu.VMEM((2, paths // 2, window // 2), jnp.bfloat16),
+            pltpu.VMEM((2, paths // 2, window // 2), jnp.bfloat16),
+            dma(hop_shape), dma(hop_shape), dma(hop_shape), dma(hop_shape),
+            dma((steps, 2 * rows)), dma((steps, 2 * rows)),
+            dma((steps + 3,)), dma((steps + 3,)),
+        ],
+        compiler_params=pltpu.CompilerParams(
+            collective_id=0, has_side_effects=True, vmem_limit_bytes=48 * 1024 * 1024
+        ),
+    )(
+        x_train, targets[None, :], noise_draws.T, alpha_init.T, velocity_init.T, frequencies,
+        phases[None, :], path_weights.T, x_window, counts,
+    )
+    return alpha.T, velocity.T, prior
+
+
 def solution(mesh):
+    def body(*args):
+        share = args[7].shape[1] // mesh.shape["row"]
+        fits = share % 16 == 0 and mesh.shape["col"] == 2 and mesh.shape["row"] % 4 == 0
+        return (fused_shards if fits and args[9].shape[0] >= 3 else shards)(*args)
+
     placed = (
         P(None, "col"),
         P("col"),
@@ -157,7 +497,7 @@
         P(),
     )
     return jax.shard_map(
-        shards,
+        body,
         mesh=mesh,
         in_specs=placed,
         out_specs=(P("col", "row"), P("col", "row"), P("col", "row")),

time: 270 us -> 118 us (0.44)
  waiting for transfers between devices: 147 us -> 0 us
  Pallas kernels: 32.6 us -> 109 us
  blocking collectives: 34.8 us -> 0 us
  matrix products: 24.8 us -> 2.43 us
  between operations: 14.3 us -> 0.79 us
  starting transfers between devices: 5.92 us -> 0 us
  other arithmetic: 5.47 us -> 1.14 us
    all_gather x3 -> x0, waiting for transfers between devices: 96.5 us -> none  [shards(): lax.all_gather(dual.astype(jnp.bfloat16), 'row', axis=0, tiled=True)]
    pallas_call x2 -> x1, Pallas kernels: 32.6 us -> 109 us  [fused_shards(): pl.pallas_call(functools.partial(fused_kernel, coeffs, steps, rows), in_s...]
    reduce_scatter x4 -> x0, waiting for transfers between devices: 43.2 us -> none  [the longest x3 27 us: shards(): mine_sums = lax.psum_scatter(sums, 'col', scatter_dimension=1, tiled=True)]
    all_to_all x2 -> x0, blocking collectives: 29.1 us -> none  [shards(): lax.all_to_all(mine_sums, 'row', split_axis=0, concat_axis=1, tiled=True)]
    dot_general x4 -> x0, matrix products: 22.4 us -> none  [the longest x3 14.7 us: shards(): jnp.dot(coeffs, kernel_tile, preferred_element_type=jnp.float32)]
    all_to_all x1 -> x0, waiting for transfers between devices: 7.27 us -> none  [shards(): lax.all_to_all(mine_sums, 'row', split_axis=0, concat_axis=1, tiled=True)]
    all_gather x1 -> x0, blocking collectives: 5.63 us -> none  [shards(): points = lax.all_gather(mine, 'col', axis=1, tiled=True)]
    all_to_all x1 -> x0, starting transfers between devices: 5.63 us -> none  [shards(): lax.all_to_all(mine_sums, 'row', split_axis=0, concat_axis=1, tiled=True)]
  transfers between devices with their start and end apart: 8 -> 0, of which waited for: 7 -> 0; matrix products, arithmetic and copies ran while one was open for 6% -> 0% of each run, Pallas kernels for 12% -> 0%
where the time goes in v2:
time: 118 us
  Pallas kernels  109 us (92%)
  local copies, waits for them, and re-layouts  4.07 us (3%)
  matrix products  2.43 us (2%)
    pallas_call x1, Pallas kernels, fused_shards(): pl.pallas_call(functools.partial(fused_kernel, coeffs, steps, rows), in_s...  109 us
    unnamed x21, local copies, waits for them, and re-layouts  4.07 us
    dot_general x1, matrix products, point_counts(): lax.dot_general(high.astype(jnp.bfloat16), low.astype(jnp.bfloat16), (((2...  2.43 us

profile of v2, /device:TPU:0, one launch (start us, length us, event | category | flops | bytes accessed | tf_op | source)
XLA Modules:
  0.0 117.9 jit_solution(1001927848771852885)
XLA Ops:
  0.6 1.1 add_select_fusion.1
  1.8 2.4 %fusion.3 = f32[1,3,32,128]{3,2,1,0:T(8,128)S(1)} fusion(s32[3,8192]{1,0:T(4,128)S(1)} %get-tuple-element.10, s32[3,8192]{1,0:T(4,128)S(1)} %get-tuple-element.9), kind=kOutput, calls=%fused_computation.5 | convolution fusion | flops 205258752 | bytes 245760 | tf_op jit(solution)/shard_map/dot_general | solution.py:93
  4.3 0.0 copy-start
  4.3 0.0 copy-start.1
  4.3 0.0 copy-start.2
  4.3 0.0 copy-start.3
  4.3 0.0 copy-start.4
  4.3 0.0 copy-start.5
  4.3 0.0 copy-start.6
  4.3 0.0 copy-start.7
  4.3 1.6 %copy.13 = bf16[2048,256]{0,1:T(8,128)(2,1)S(1)} copy(bf16[2048,256]{1,0:T(8,128)(2,1)} %param.17) | data formatting | bytes 2097152 | tf_op args[7]
  6.0 0.0 copy-done
  6.0 0.0 copy-done.1
  6.0 0.0 copy-done.2
  6.0 0.0 copy-done.3
  6.0 0.0 copy-done.4
  6.0 0.0 copy-done.5
  6.0 0.0 copy-done.6
  6.0 0.0 copy-done.7
  6.0 109.5 %shard_map.121 = (f32[16,4096]{1,0:T(8,128)S(1)}, f32[16,4096]{1,0:T(8,128)S(1)}, f32[128,2048]{1,0:T(8,128)S(1)}) custom-call(bf16[64,4096]{1,0:T(8,128)(2,1)S(1)} %copy-done, f32[1,4096]{1,0:T(1,128)S(1)} %bitcast.20, f32[16,4096]{1,0:T(8,128)S(1)} %bitcast.14, f32[16,4096]{1,0:T(8,128)S(1)} %bitcast.15, f32[16,4096]{1,0:T(8,128)S(1)} %bitcast.16, ...), custom_call_target="tpu_custom_call" | custom-call | tf_op jit(solution)/shard_map/pallas_call | solution.py:445
  115.5 0.7 copy.20
  116.2 0.7 copy.21
  116.9 1.0 copy.22
  (1 shorter events, 0.0 us)
Async XLA Ops:
  4.3 1.7 %copy-start = (bf16[64,4096]{1,0:T(8,128)(2,1)S(1)}, bf16[64,4096]{1,0:T(8,128)(2,1)}, u32[]{:S(2)}) copy-start(bf16[64,4096]{1,0:T(8,128)(2,1)} %x_ref.1) | copy-start | bytes 1572868
  4.3 1.7 %copy-start.1 = (f32[4096,16]{0,1:T(8,128)S(1)}, f32[4096,16]{0,1:T(8,128)}, u32[]{:S(2)}) copy-start(f32[4096,16]{0,1:T(8,128)} %param.12) | copy-start | bytes 786436
  4.3 1.7 %copy-start.2 = (f32[4096,16]{0,1:T(8,128)S(1)}, f32[4096,16]{0,1:T(8,128)}, u32[]{:S(2)}) copy-start(f32[4096,16]{0,1:T(8,128)} %param.13) | copy-start | bytes 786436
  4.3 1.7 %copy-start.3 = (f32[4096,16]{0,1:T(8,128)S(1)}, f32[4096,16]{0,1:T(8,128)}, u32[]{:S(2)}) copy-start(f32[4096,16]{0,1:T(8,128)} %param.14) | copy-start | bytes 786436
  4.3 1.7 %copy-start.4 = (bf16[64,2048]{1,0:T(8,128)(2,1)S(1)}, bf16[64,2048]{1,0:T(8,128)(2,1)}, u32[]{:S(2)}) copy-start(bf16[64,2048]{1,0:T(8,128)(2,1)} %freq_ref.1) | copy-start | bytes 786436
  4.3 1.7 %copy-start.5 = (bf16[64,2048]{1,0:T(8,128)(2,1)S(1)}, bf16[64,2048]{1,0:T(8,128)(2,1)}, u32[]{:S(2)}) copy-start(bf16[64,2048]{1,0:T(8,128)(2,1)} %window_ref.1) | copy-start | bytes 786436
  4.3 1.7 %copy-start.6 = (f32[4096]{0:T(1024)S(1)}, f32[4096]{0:T(1024)}, u32[]{:S(2)}) copy-start(f32[4096]{0:T(1024)} %param.11) | copy-start | bytes 49156
  4.3 1.7 %copy-start.7 = (f32[2048]{0:T(1024)S(1)}, f32[2048]{0:T(1024)}, u32[]{:S(2)}) copy-start(f32[2048]{0:T(1024)} %param.16) | copy-start | bytes 24580

commit v3 on v2

--- a/solution.py
+++ b/solution.py
@@ -148,8 +148,8 @@
 
 def fused_kernel(
     scale_coeffs, steps, rows, x_ref, target_ref, noise_ref, alpha_in, velocity_in, freq_ref,
-    phase_ref, weight_ref, window_ref, count_ref, alpha_ref, velocity_ref, prior_ref,
-    gathered, tile, train_prior, points, points_t, base, outboxes, arrivals, last_outbox, last_arrived,
+    phase_ref, weight_ref, window_ref, index_ref, alpha_ref, velocity_ref, prior_ref,
+    count_ref, gathered, tile, train_prior, points, points_t, base, outboxes, arrivals, last_outbox, last_arrived,
     window_out, window_in,
     ring_send, ring_recv, pair_send, pair_recv, sum_send, sum_recv, misc_send, misc_recv,
 ):
@@ -345,6 +345,17 @@
 
         lax.fori_loop(0, 2 * own // group, rows_of, 0)
 
+    def count_points(step):
+        lanes = 128
+        local = index_ref[step : step + 1, :] - col * train
+        high_ids = lax.broadcasted_iota(jnp.int32, (train // lanes, 1), 0)
+        low_ids = lax.broadcasted_iota(jnp.int32, (lanes, 1), 0)
+        high = ((local >> 7) == high_ids).astype(jnp.float32).astype(jnp.bfloat16)
+        low = ((local & 127) == low_ids).astype(jnp.float32).astype(jnp.bfloat16)
+        table = against(high, low)
+        for i in range(train // lanes):
+            count_ref[step : step + 1, i * lanes : (i + 1) * lanes] = table[i : i + 1, :]
+
     tiles = 2 * events
     wide = window_ref.shape[1] // tiles
 
@@ -395,6 +406,8 @@
             pl.ds(pl.multiple_of(col * own, own), own),
         ]
 
+        count_points(step)
+
         def receive(d, carry):
             sum_copy(step, d).wait_recv()
             return carry
@@ -437,7 +450,6 @@
     share = paths // rows
     own = train // rows
     window = x_window.shape[1]
-    counts = point_counts(batch_index, lax.axis_index("col") * train, train)
     coeffs = sine_coeffs((2.0 / (frequencies.shape[1] * col_count)) ** 0.5)
     vmem = pl.BlockSpec(memory_space=pltpu.VMEM)
     dma = pltpu.SemaphoreType.DMA
@@ -452,6 +464,7 @@
             jax.ShapeDtypeStruct((paths // 2, window), jnp.float32),
         ),
         scratch_shapes=[
+            pltpu.VMEM((steps, train), jnp.float32),
             pltpu.VMEM((steps, paths, train), jnp.bfloat16),
             pltpu.VMEM((2 * own, train), jnp.bfloat16),
             pltpu.VMEM((paths, 2 * own), jnp.float32),
@@ -473,7 +486,7 @@
         ),
     )(
         x_train, targets[None, :], noise_draws.T, alpha_init.T, velocity_init.T, frequencies,
-        phases[None, :], path_weights.T, x_window, counts,
+        phases[None, :], path_weights.T, x_window, batch_index,
     )
     return alpha.T, velocity.T, prior
 

time: 118 us -> 116 us (0.983)
  matrix products: 2.43 us -> 0 us
  Pallas kernels: 109 us -> 111 us
    dot_general x1 -> x0, matrix products: 2.43 us -> none  [point_counts(): lax.dot_general(high.astype(jnp.bfloat16), low.astype(jnp.bfloat16), (((2...]
    unnamed x21 -> x22, local copies, waits for them, and re-layouts: 4.07 us -> 4.03 us
where the time goes in v3:
time: 116 us; the launch traced here: 115 us
  Pallas kernels  111 us (96%)
  local copies, waits for them, and re-layouts  4.03 us (3%)
    pallas_call x1, Pallas kernels, fused_shards(): pl.pallas_call(functools.partial(fused_kernel, coeffs, steps, rows), in_s...  111 us
    unnamed x22, local copies, waits for them, and re-layouts  4.03 us

profile of v3, /device:TPU:0, one launch (start us, length us, event | category | flops | bytes accessed | tf_op | source)
XLA Modules:
  0.0 115.4 jit_solution(12005054185972532806)
XLA Ops:
  0.6 0.0 copy-start
  0.6 0.0 copy-start.1
  0.7 0.0 copy-start.2
  0.7 0.0 copy-start.3
  0.7 0.0 copy-start.4
  0.7 0.0 copy-start.5
  0.7 0.0 copy-start.6
  0.7 0.0 copy-start.7
  0.7 0.0 copy-start.8
  0.7 1.6 %copy.13 = bf16[2048,256]{0,1:T(8,128)(2,1)S(1)} copy(bf16[2048,256]{1,0:T(8,128)(2,1)} %param.17) | data formatting | bytes 2097152 | tf_op args[7]
  2.3 0.0 copy-done
  2.4 0.0 copy-done.1
  2.4 0.0 copy-done.2
  2.4 0.0 copy-done.3
  2.4 0.0 copy-done.4
  2.4 0.0 copy-done.5
  2.4 0.0 copy-done.6
  2.4 0.0 copy-done.7
  2.4 0.0 copy-done.8
  2.4 110.6 %shard_map.121 = (f32[16,4096]{1,0:T(8,128)S(1)}, f32[16,4096]{1,0:T(8,128)S(1)}, f32[128,2048]{1,0:T(8,128)S(1)}) custom-call(bf16[64,4096]{1,0:T(8,128)(2,1)S(1)} %copy-done, f32[1,4096]{1,0:T(1,128)S(1)} %bitcast.14, f32[16,4096]{1,0:T(8,128)S(1)} %bitcast.9, f32[16,4096]{1,0:T(8,128)S(1)} %bitcast.10, f32[16,4096]{1,0:T(8,128)S(1)} %bitcast.11, ...), custom_call_target="tpu_custom_call" | custom-call | tf_op jit(solution)/shard_map/pallas_call | solution.py:457
  113.0 0.7 copy.17
  113.7 0.7 copy.18
  114.5 1.0 copy.19
Async XLA Ops:
  0.6 1.7 %copy-start = (bf16[64,4096]{1,0:T(8,128)(2,1)S(1)}, bf16[64,4096]{1,0:T(8,128)(2,1)}, u32[]{:S(2)}) copy-start(bf16[64,4096]{1,0:T(8,128)(2,1)} %x_ref.1) | copy-start | bytes 1572868
  0.6 1.7 %copy-start.1 = (f32[4096,16]{0,1:T(8,128)S(1)}, f32[4096,16]{0,1:T(8,128)}, u32[]{:S(2)}) copy-start(f32[4096,16]{0,1:T(8,128)} %param.12) | copy-start | bytes 786436
  0.7 1.7 %copy-start.2 = (f32[4096,16]{0,1:T(8,128)S(1)}, f32[4096,16]{0,1:T(8,128)}, u32[]{:S(2)}) copy-start(f32[4096,16]{0,1:T(8,128)} %param.13) | copy-start | bytes 786436
  0.7 1.7 %copy-start.3 = (f32[4096,16]{0,1:T(8,128)S(1)}, f32[4096,16]{0,1:T(8,128)}, u32[]{:S(2)}) copy-start(f32[4096,16]{0,1:T(8,128)} %param.14) | copy-start | bytes 786436
  0.7 1.7 %copy-start.4 = (bf16[64,2048]{1,0:T(8,128)(2,1)S(1)}, bf16[64,2048]{1,0:T(8,128)(2,1)}, u32[]{:S(2)}) copy-start(bf16[64,2048]{1,0:T(8,128)(2,1)} %freq_ref.1) | copy-start | bytes 786436
  0.7 1.7 %copy-start.5 = (bf16[64,2048]{1,0:T(8,128)(2,1)S(1)}, bf16[64,2048]{1,0:T(8,128)(2,1)}, u32[]{:S(2)}) copy-start(bf16[64,2048]{1,0:T(8,128)(2,1)} %window_ref.1) | copy-start | bytes 786436
  0.7 1.7 %copy-start.6 = (s32[3,8192]{1,0:T(4,128)S(1)}, s32[3,8192]{1,0:T(4,128)}, u32[]{:S(2)}) copy-start(s32[3,8192]{1,0:T(4,128)} %index_ref.1) | copy-start | bytes 294916
  0.7 1.7 %copy-start.7 = (f32[4096]{0:T(1024)S(1)}, f32[4096]{0:T(1024)}, u32[]{:S(2)}) copy-start(f32[4096]{0:T(1024)} %param.11) | copy-start | bytes 49156
  0.7 1.7 %copy-start.8 = (f32[2048]{0:T(1024)S(1)}, f32[2048]{0:T(1024)}, u32[]{:S(2)}) copy-start(f32[2048]{0:T(1024)} %param.16) | copy-start | bytes 24580
